TPU v7x, 32 devices: a whole 2x2x4 slice. The times are simulated.
32 devices in a mesh: dp: 8 (over z, y), tensor: 4 (over x, core).
Axes of the slice: x: 2, y: 2, z: 4, core: 2. Of those that a mesh axis runs over, the one named last changes fastest.
Arguments:
- tokens: bfloat16 [8192, 2048], P('dp'), may hold values from -6 to 6
- segment_ids: int32 [8, 1024], P('dp'), may hold values from 0 to 7, never falling along the last dimension, each value on 1 to 512 neighbouring positions
- attn_gain: bfloat16 [2048], P('dp'), may hold values from 0.25 to 1.75
- query_weight: bfloat16 [2048, 2048], P('dp', 'tensor'), may hold values from -0.125 to 0.125
- key_weight: bfloat16 [2048, 512], P('dp', 'tensor'), may hold values from -0.125 to 0.125
- value_weight: bfloat16 [2048, 512], P('dp', 'tensor'), may hold values from -0.125 to 0.125
- output_weight: bfloat16 [2048, 2048], P('tensor', 'dp'), may hold values from -0.5 to 0.5
- ffn_gain: bfloat16 [2048], P('dp'), may hold values from 0.25 to 1.75
- gate_weight: bfloat16 [2048, 8192], P('dp', 'tensor'), may hold values from -0.125 to 0.125
- up_weight: bfloat16 [2048, 8192], P('dp', 'tensor'), may hold values from -0.125 to 0.125
- down_weight: bfloat16 [8192, 2048], P('tensor', 'dp'), may hold values from -0.0625 to 0.0625
- cotangent: bfloat16 [8192, 2048], P('dp'), may hold values from -6 to 6
Outputs:
- layer_output: bfloat16 [8192, 2048], P('dp')
- tokens_grad: float32 [8192, 2048], P('dp')
- attn_gain_grad: float32 [2048], P('dp')
- query_weight_grad: float32 [2048, 2048], P('dp', 'tensor')
- key_weight_grad: float32 [2048, 512], P('dp', 'tensor')
- value_weight_grad: float32 [2048, 512], P('dp', 'tensor')
- output_weight_grad: float32 [2048, 2048], P('tensor', 'dp')
- ffn_gain_grad: float32 [2048], P('dp')
- gate_weight_grad: float32 [2048, 8192], P('dp', 'tensor')
- up_weight_grad: float32 [2048, 8192], P('dp', 'tensor')
- down_weight_grad: float32 [8192, 2048], P('tensor', 'dp')
Inputs may be any that keep to these rules, and one draw needn't show every extreme that they name: In each row of segment_ids the numbers never fall; each document spans 1 to 512 positions, and one spans exactly 512.
All inputs are finite; a program needn't handle non-finite values.
Results may differ from a plain program's by a relative error of at most 0.02.
Values may be sent and summed in bfloat16 or wider, within the bound.
A program may use at most 256 MiB of HBM per device.

v0:
```python
from functools import partial
import math
import jax
import jax.numpy as jnp
from jax import lax
from jax.sharding import PartitionSpec as P

HD = 64
epsilon = 1e-05


def rope_tables(segment_row, head_size):
    length = segment_row.shape[0]
    places = jnp.arange(length, dtype=jnp.int32)
    boundary = jnp.concatenate([jnp.ones((1,), dtype=bool), segment_row[1:] != segment_row[:-1]])
    starts = lax.cummax(jnp.where(boundary, places, 0), axis=0)
    position = (places - starts).astype(jnp.float32)
    half_size = head_size // 2
    exponent = jnp.arange(half_size, dtype=jnp.float32) * 2.0 / head_size
    inverse = 1.0 / 500000.0**exponent
    wavelen = 2.0 * math.pi / inverse
    smooth = (8192.0 / wavelen - 1.0) / 3.0
    scaled = jnp.where(
        wavelen < 2048.0,
        inverse,
        jnp.where(
            wavelen > 8192.0, inverse / 32.0, (1.0 - smooth) * inverse / 32.0 + smooth * inverse
        ),
    )
    angles = position[:, None] * scaled[None, :]
    cosine_table = jnp.cos(angles)
    sine_table = jnp.sin(angles)
    return (
        jnp.concatenate([cosine_table, cosine_table], axis=-1),
        jnp.concatenate([sine_table, sine_table], axis=-1),
    )


def rotate(values, cosine_table, sine_table):
    half_size = values.shape[-1] // 2
    turned = jnp.concatenate([-values[..., half_size:], values[..., :half_size]], axis=-1)
    return values * cosine_table + turned * sine_table


def rms_norm(values, gain_vector):
    factor = lax.rsqrt(jnp.mean(values * values, axis=-1, keepdims=True) + epsilon)
    return values * factor * gain_vector


def swiglu(gate_values, up_values):
    return jax.nn.silu(gate_values) * up_values


def contract_rows(left_side, right_side):
    return lax.dot_general(
        left_side, right_side, (((0,), (0,)), ((), ())), preferred_element_type=jnp.float32
    )


def contract_cols(left_side, right_side):
    return lax.dot_general(
        left_side, right_side, (((1,), (1,)), ((), ())), preferred_element_type=jnp.float32
    )


def block_scores(query_block, key_seq, segment_row, start_row):
    row_count = query_block.shape[0]
    length = key_seq.shape[0]
    score_scale = query_block.shape[-1] ** (-0.5)
    scores = (
        jnp.einsum("qkgd,skd->kgqs", query_block, key_seq, preferred_element_type=jnp.float32)
        * score_scale
    )
    row_ids = start_row + jnp.arange(row_count, dtype=jnp.int32)
    col_ids = jnp.arange(length, dtype=jnp.int32)
    same_doc = segment_row[start_row : start_row + row_count][:, None] == segment_row[None, :]
    allowed = same_doc & (col_ids[None, :] <= row_ids[:, None])
    return jnp.where(allowed, scores, -1000000000.0)


def attend_forward(operands):
    query_seq, key_seq, value_seq, segment_row = operands
    length, kv_local, head_size = key_seq.shape
    grouped = query_seq.reshape(length, kv_local, -1, head_size)
    block_rows = min(512, length)
    mixed_parts = []
    total_parts = []
    for start_row in range(0, length, block_rows):
        scores = block_scores(
            grouped[start_row : start_row + block_rows], key_seq, segment_row, start_row
        )
        row_max = jnp.max(scores, axis=-1, keepdims=True)
        log_total = jnp.log(jnp.sum(jnp.exp(scores - row_max), axis=-1, keepdims=True)) + row_max
        soft_low = jnp.exp(scores - log_total).astype(jnp.bfloat16)
        mixed_block = jnp.einsum(
            "kgqs,skd->qkgd", soft_low, value_seq, preferred_element_type=jnp.float32
        )
        mixed_parts.append(mixed_block.reshape(block_rows, -1).astype(jnp.bfloat16))
        total_parts.append(log_total)
    return (jnp.concatenate(mixed_parts, axis=0), jnp.concatenate(total_parts, axis=2))


def attend_backward(operands):
    query_seq, key_seq, value_seq, log_total, grad_seq, segment_row = operands
    length, kv_local, head_size = key_seq.shape
    grouped = query_seq.reshape(length, kv_local, -1, head_size)
    grad_grouped = grad_seq.reshape(length, kv_local, -1, head_size)
    block_rows = min(512, length)
    score_scale = head_size ** (-0.5)
    query_parts = []
    key_grad = jnp.zeros(key_seq.shape, jnp.float32)
    value_grad = jnp.zeros(value_seq.shape, jnp.float32)
    for start_row in range(0, length, block_rows):
        query_block = grouped[start_row : start_row + block_rows]
        grad_block = grad_grouped[start_row : start_row + block_rows]
        scores = block_scores(query_block, key_seq, segment_row, start_row)
        soft_weights = jnp.exp(scores - log_total[:, :, start_row : start_row + block_rows])
        soft_grad = jnp.einsum(
            "qkgd,skd->kgqs", grad_block, value_seq, preferred_element_type=jnp.float32
        )
        score_grad = (
            soft_weights * (soft_grad - jnp.sum(soft_weights * soft_grad, axis=-1, keepdims=True))
        ).astype(jnp.bfloat16)
        query_parts.append(
            jnp.einsum("kgqs,skd->qkgd", score_grad, key_seq, preferred_element_type=jnp.float32)
            * score_scale
        )
        key_grad = (
            key_grad
            + jnp.einsum(
                "kgqs,qkgd->skd", score_grad, query_block, preferred_element_type=jnp.float32
            )
            * score_scale
        )
        value_grad = value_grad + jnp.einsum(
            "kgqs,qkgd->skd",
            soft_weights.astype(jnp.bfloat16),
            grad_block,
            preferred_element_type=jnp.float32,
        )
    query_grad = jnp.concatenate(query_parts, axis=0).reshape(length, -1, head_size)
    return (query_grad, key_grad, value_grad)


def shards(
    tokens,
    segment_ids,
    attn_gain,
    query_weight,
    key_weight,
    value_weight,
    output_weight,
    ffn_gain,
    gate_weight,
    up_weight,
    down_weight,
    cotangent,
):
    gathered = (
        lax.all_gather(attn_gain, "dp", axis=0, tiled=True),
        lax.all_gather(query_weight, "dp", axis=0, tiled=True),
        lax.all_gather(key_weight, "dp", axis=0, tiled=True),
        lax.all_gather(value_weight, "dp", axis=0, tiled=True),
        lax.all_gather(output_weight, "dp", axis=1, tiled=True),
        lax.all_gather(ffn_gain, "dp", axis=0, tiled=True),
        lax.all_gather(gate_weight, "dp", axis=0, tiled=True),
        lax.all_gather(up_weight, "dp", axis=0, tiled=True),
        lax.all_gather(down_weight, "dp", axis=1, tiled=True),
    )
    seq_count, length = segment_ids.shape
    token_count = tokens.shape[0]
    tokens_float = tokens.astype(jnp.float32)
    cotangent_float = cotangent.astype(jnp.float32)
    attn_scale = gathered[0].astype(jnp.float32)
    ffn_scale = gathered[5].astype(jnp.float32)
    normed = rms_norm(tokens_float, attn_scale).astype(jnp.bfloat16)
    query_raw = jnp.dot(normed, gathered[1], preferred_element_type=jnp.float32)
    key_raw = jnp.dot(normed, gathered[2], preferred_element_type=jnp.float32)
    value_low = jnp.dot(normed, gathered[3], preferred_element_type=jnp.float32).astype(
        jnp.bfloat16
    )
    cosine_table, sine_table = jax.vmap(partial(rope_tables, head_size=HD))(segment_ids)
    cosine_wide = cosine_table[:, :, None, :]
    sine_wide = sine_table[:, :, None, :]
    query_shaped = query_raw.reshape(seq_count, length, -1, HD)
    key_shaped = key_raw.reshape(seq_count, length, -1, HD)
    query_low = rotate(query_shaped, cosine_wide, sine_wide).astype(jnp.bfloat16)
    key_low = rotate(key_shaped, cosine_wide, sine_wide).astype(jnp.bfloat16)
    value_seqs = value_low.reshape(seq_count, length, -1, HD)
    mixed_low, log_total = lax.map(attend_forward, (query_low, key_low, value_seqs, segment_ids))
    mixed_low = mixed_low.reshape(token_count, -1)
    attn_part = jnp.dot(mixed_low, gathered[4], preferred_element_type=jnp.float32)
    hidden_state = tokens_float + lax.psum(attn_part, "tensor")
    normed_two = rms_norm(hidden_state, ffn_scale).astype(jnp.bfloat16)
    gate_values = jnp.dot(normed_two, gathered[6], preferred_element_type=jnp.float32)
    up_values = jnp.dot(normed_two, gathered[7], preferred_element_type=jnp.float32)
    active = swiglu(gate_values, up_values).astype(jnp.bfloat16)
    ffn_part = jnp.dot(active, gathered[8], preferred_element_type=jnp.float32)
    layer_output = (
        hidden_state + lax.psum(ffn_part.astype(jnp.bfloat16), "tensor").astype(jnp.float32)
    ).astype(jnp.bfloat16)
    down_grad = contract_rows(active, cotangent)
    active_grad = contract_cols(cotangent, gathered[8])
    unused_value, swiglu_pull = jax.vjp(swiglu, gate_values, up_values)
    gate_grad, up_grad = swiglu_pull(active_grad)
    gate_low = gate_grad.astype(jnp.bfloat16)
    up_low = up_grad.astype(jnp.bfloat16)
    gate_weight_grad = contract_rows(normed_two, gate_low)
    up_weight_grad = contract_rows(normed_two, up_low)
    mlp_part = contract_cols(gate_low, gathered[6]) + contract_cols(up_low, gathered[7])
    normed_two_grad = lax.psum(mlp_part, "tensor")
    unused_second, second_pull = jax.vjp(rms_norm, hidden_state, ffn_scale)
    hidden_part, ffn_gain_grad = second_pull(normed_two_grad)
    hidden_grad = cotangent_float + hidden_part
    hidden_low = hidden_grad.astype(jnp.bfloat16)
    output_weight_grad = contract_rows(mixed_low, hidden_low)
    mixed_grad = contract_cols(hidden_low, gathered[4]).astype(jnp.bfloat16)
    query_grad, key_grad, value_grad = lax.map(
        attend_backward,
        (
            query_low,
            key_low,
            value_seqs,
            log_total,
            mixed_grad.reshape(seq_count, length, -1, HD),
            segment_ids,
        ),
    )
    unused_query, query_pull = jax.vjp(
        partial(rotate, cosine_table=cosine_wide, sine_table=sine_wide), query_shaped
    )
    unused_key, key_pull = jax.vjp(
        partial(rotate, cosine_table=cosine_wide, sine_table=sine_wide), key_shaped
    )
    query_raw_grad = query_pull(query_grad)[0].reshape(token_count, -1).astype(jnp.bfloat16)
    key_raw_grad = key_pull(key_grad)[0].reshape(token_count, -1).astype(jnp.bfloat16)
    value_raw_grad = value_grad.reshape(token_count, -1).astype(jnp.bfloat16)
    query_weight_grad = contract_rows(normed, query_raw_grad)
    key_weight_grad = contract_rows(normed, key_raw_grad)
    value_weight_grad = contract_rows(normed, value_raw_grad)
    attn_back_part = (
        contract_cols(query_raw_grad, gathered[1])
        + contract_cols(key_raw_grad, gathered[2])
        + contract_cols(value_raw_grad, gathered[3])
    )
    normed_grad = lax.psum(attn_back_part.astype(jnp.bfloat16), "tensor").astype(jnp.float32)
    unused_first, first_pull = jax.vjp(rms_norm, tokens_float, attn_scale)
    token_part, attn_gain_grad = first_pull(normed_grad)
    tokens_grad = hidden_grad + token_part
    summed = (
        lax.psum_scatter(
            attn_gain_grad.astype(jnp.bfloat16), "dp", scatter_dimension=0, tiled=True
        ).astype(jnp.float32),
        lax.psum_scatter(
            query_weight_grad.astype(jnp.bfloat16), "dp", scatter_dimension=0, tiled=True
        ).astype(jnp.float32),
        lax.psum_scatter(
            key_weight_grad.astype(jnp.bfloat16), "dp", scatter_dimension=0, tiled=True
        ).astype(jnp.float32),
        lax.psum_scatter(
            value_weight_grad.astype(jnp.bfloat16), "dp", scatter_dimension=0, tiled=True
        ).astype(jnp.float32),
        lax.psum_scatter(
            output_weight_grad.astype(jnp.bfloat16), "dp", scatter_dimension=1, tiled=True
        ).astype(jnp.float32),
        lax.psum_scatter(
            ffn_gain_grad.astype(jnp.bfloat16), "dp", scatter_dimension=0, tiled=True
        ).astype(jnp.float32),
        lax.psum_scatter(
            gate_weight_grad.astype(jnp.bfloat16), "dp", scatter_dimension=0, tiled=True
        ).astype(jnp.float32),
        lax.psum_scatter(
            up_weight_grad.astype(jnp.bfloat16), "dp", scatter_dimension=0, tiled=True
        ).astype(jnp.float32),
        lax.psum_scatter(
            down_grad.astype(jnp.bfloat16), "dp", scatter_dimension=1, tiled=True
        ).astype(jnp.float32),
    )
    attn_gain_total = summed[0]
    ffn_gain_total = summed[5]
    return (
        layer_output,
        tokens_grad,
        attn_gain_total,
        summed[1],
        summed[2],
        summed[3],
        summed[4],
        ffn_gain_total,
        summed[6],
        summed[7],
        summed[8],
    )


def solution(mesh):
    return jax.shard_map(
        shards,
        mesh=mesh,
        in_specs=(
            P("dp", None),
            P("dp", None),
            P("dp"),
            P("dp", "tensor"),
            P("dp", "tensor"),
            P("dp", "tensor"),
            P("tensor", "dp"),
            P("dp"),
            P("dp", "tensor"),
            P("dp", "tensor"),
            P("tensor", "dp"),
            P("dp", None),
        ),
        out_specs=(
            P("dp", None),
            P("dp", None),
            P("dp"),
            P("dp", "tensor"),
            P("dp", "tensor"),
            P("dp", "tensor"),
            P("tensor", "dp"),
            P("dp"),
            P("dp", "tensor"),
            P("dp", "tensor"),
            P("tensor", "dp"),
        ),
        check_vma=False,
    )
```

profile of v0, /device:TPU:0, one launch (start us, length us, event | category | flops | bytes accessed | tf_op | source)
XLA Modules:
  0.0 1853.7 jit_solution(15969643140244901022)
XLA Ops:
  15.5 22.5 %all-gather = bf16[8,1,256]{2,1,0:T(2,128)(2,1)S(1)} all-gather(bf16[1,1,256]{2,1,0:T(2,128)(2,1)S(1)} %reshape.443), channel_id=1, replica_groups=mesh['dp'=8,'tensor'=4] {'dp'}, dimensions={0}, use_global_device_ids=true | all-gather | bytes 4608 | tf_op jit(solution)/shard_map/all_gather | solution.py:160
  38.7 33.1 %all_gather.29 = bf16[2048,128]{1,0:T(8,128)(2,1)S(1)} all-gather(bf16[256,128]{1,0:T(8,128)(2,1)} %param.16), channel_id=1, replica_groups=mesh['dp'=8,'tensor'=4] {'dp'}, dimensions={0}, use_global_device_ids=true | all-gather | bytes 589824 | tf_op jit(solution)/shard_map/all_gather | solution.py:162
  71.8 32.3 %all_gather.28 = bf16[2048,128]{1,0:T(8,128)(2,1)S(1)} all-gather(bf16[256,128]{1,0:T(8,128)(2,1)} %param.17), channel_id=1, replica_groups=mesh['dp'=8,'tensor'=4] {'dp'}, dimensions={0}, use_global_device_ids=true | all-gather | bytes 589824 | tf_op jit(solution)/shard_map/all_gather | solution.py:163
  126.0 9.2 exponential_reduce_fusion
  142.6 9.2 exponential_reduce_fusion.1
  176.0 16.3 all-gather.1
  192.3 132.1 %all-reduce.12.cloned.1.call-done = f32[1024,2048]{1,0:T(8,128)} async-done(((f32[1024,2048]{1,0:T(8,128)}), f32[1024,2048]{1,0:T(8,128)}) %all-reduce.12.cloned.1.call-update) | async-done | bytes 8388624 | tf_op jit(solution)/shard_map/psum | solution.py:193
  336.3 114.8 %all-gather.14.cloned.1.call-done = bf16[2048,2048]{1,0:T(8,128)(2,1)} async-done(((bf16[256,2048]{1,0:T(8,128)(2,1)}), bf16[2048,2048]{1,0:T(8,128)(2,1)}) %all-gather.14.cloned.1.call-update) | async-done | bytes 8388624 | tf_op jit(solution)/shard_map/all_gather | solution.py:167
  451.1 14.7 fusion.66
  465.8 110.0 %all-gather.12.cloned.1.call-done = bf16[2048,2048]{1,0:T(8,128)(2,1)} async-done(((bf16[256,2048]{1,0:T(8,128)(2,1)}), bf16[2048,2048]{1,0:T(8,128)(2,1)}) %all-gather.12.cloned.1.call-update) | async-done | bytes 8388624 | tf_op jit(solution)/shard_map/all_gather | solution.py:166
  575.8 14.6 fusion.65
  590.3 110.5 %all-gather.16.cloned.1.call-done = bf16[2048,2048]{1,0:T(8,128)(2,1)} async-done(((bf16[2048,256]{1,0:T(8,128)(2,1)}), bf16[2048,2048]{1,0:T(8,128)(2,1)}) %all-gather.16.cloned.1.call-update) | async-done | bytes 8388624 | tf_op jit(solution)/shard_map/all_gather | solution.py:168
  700.8 21.7 %multiply_convert_fusion = (bf16[1024,2048]{1,0:T(8,128)(2,1)}, bf16[1024,2048]{1,0:T(8,128)(2,1)}, bf16[1024,2048]{1,0:T(8,128)(2,1)}) fusion(f32[1024,2048]{1,0:T(8,128)} %fusion.65, f32[1024,2048]{1,0:T(8,128)} %fusion.66, bf16[1024,2048]{1,0:T(8,128)(2,1)} %param.23, bf16[2048,2048]{1,0:T(8,128)(2,1)} %all-gather.16.cloned.1.call-done), kind=kOutput, calls=%fused_computation.44 | convolution fusion | flops 8623489024 | bytes 41943040 | tf_op jit(solution)/shard_map/dot_general | solution.py:61
  722.5 13.1 fusion.67
  735.7 13.6 convolution_add_fusion
  751.1 149.5 %all-reduce.14.cloned.1.call-done = f32[1024,2048]{1,0:T(8,128)} async-done(((f32[1024,2048]{1,0:T(8,128)}), f32[1024,2048]{1,0:T(8,128)}) %all-reduce.14.cloned.1.call-update) | async-done | bytes 8388624 | tf_op jit(solution)/shard_map/psum | solution.py:211
  908.5 9.6 fusion.17
  930.6 9.4 fusion
  940.0 13.8 fusion.3
  953.8 8.6 fusion.40
  964.7 30.0 %fusion.2 = (bf16[2,4,512,1024]{2,3,1,0:T(8,128)(2,1)}, bf16[2,4,512,1024]{2,3,1,0:T(8,128)(2,1)}) fusion(f32[2,1024,512,4]{2,1,3,0:T(8,128)} %get-tuple-element.98, f32[2,1024,512,4]{2,1,3,0:T(8,128)} %get-tuple-element.94, f32[2,4,512]{2,1,0:T(4,128)S(1)} %copy-done.35, f32[2,4,512]{2,1,0:T(4,128)S(1)} %bitcast.237, ...), kind=kLoop, calls=%fused_computation.4 | loop fusion | flops 50331648 | bytes 85000192 | tf_op jit(solution)/shard_map/while/body/eval_jaxpr/convert_element_type | solution.py:123
  1029.6 13.8 convolution_convert_fusion.3
  1051.0 14.1 convolution_convert_fusion
  1065.2 14.1 convolution_convert_fusion.1
  1079.6 14.2 convolution_convert_fusion.2
  1098.7 66.6 %reduce-scatter.14.cloned.1.call-done = bf16[512,256]{1,0:T(8,128)(2,1)} async-done(((bf16[512,2048]{1,0:T(8,128)(2,1)}), bf16[512,256]{1,0:T(8,128)(2,1)}) %reduce-scatter.14.cloned.1.call-update) | async-done | bytes 262160 | tf_op jit(solution)/shard_map/reduce_scatter | solution.py:263
  1167.0 69.8 %reduce-scatter.8.cloned.1.call-done = bf16[256,512]{1,0:T(8,128)(2,1)} async-done(((bf16[2048,512]{1,0:T(8,128)(2,1)}), bf16[256,512]{1,0:T(8,128)(2,1)}) %reduce-scatter.8.cloned.1.call-update) | async-done | bytes 262160 | tf_op jit(solution)/shard_map/reduce_scatter | solution.py:254
  1238.6 153.1 %all-reduce.16.cloned.1.call-done = (bf16[1024,2048]{1,0:T(8,128)(2,1)}, bf16[1024,2048]{1,0:T(8,128)(2,1)}) async-done(((bf16[1024,2048]{1,0:T(8,128)(2,1)}, bf16[1024,2048]{1,0:T(8,128)(2,1)}), (bf16[1024,2048]{1,0:T(8,128)(2,1)}, bf16[1024,2048]{1,0:T(8,128)(2,1)})) %all-reduce.16.cloned.1.call-update) | async-done | bytes 8388624 | tf_op jit(solution)/shard_map/psum | solution.py:200
  1397.7 22.9 %all-reduce.6 = (bf16[2048]{0:T(1024)(128)(2,1)S(1)}, bf16[2048]{0:T(1024)(128)(2,1)S(1)}) all-reduce(bf16[2048]{0:T(1024)(128)(2,1)S(1)} %get-tuple-element.54, bf16[2048]{0:T(1024)(128)(2,1)S(1)} %copy-done.41), channel_id=2, replica_groups=mesh['dp'=8,'tensor'=4] {'dp'}, use_global_device_ids=true, to_apply=%region_17.18.clone | all-reduce | flops 4096 | bytes 16384
  1437.4 106.4 %reduce-scatter.20.cloned.1.call-done = bf16[2048,256]{1,0:T(8,128)(2,1)} async-done(((bf16[2048,2048]{1,0:T(8,128)(2,1)}), bf16[2048,256]{1,0:T(8,128)(2,1)}) %reduce-scatter.20.cloned.1.call-update) | async-done | bytes 1048592 | tf_op jit(solution)/shard_map/reduce_scatter | solution.py:275
  1546.5 147.4 %reduce-scatter.18.cloned.1.call-done = bf16[256,2048]{1,0:T(8,128)(2,1)} async-done(((bf16[2048,2048]{1,0:T(8,128)(2,1)}), bf16[256,2048]{1,0:T(8,128)(2,1)}) %reduce-scatter.18.cloned.1.call-update) | async-done | bytes 1048592 | tf_op jit(solution)/shard_map/reduce_scatter | solution.py:272
  1696.7 147.3 %reduce-scatter.16.cloned.1.call-done = bf16[256,2048]{1,0:T(8,128)(2,1)} async-done(((bf16[2048,2048]{1,0:T(8,128)(2,1)}), bf16[256,2048]{1,0:T(8,128)(2,1)}) %reduce-scatter.16.cloned.1.call-update) | async-done | bytes 1048592 | tf_op jit(solution)/shard_map/reduce_scatter | solution.py:269
  (226 shorter events, 179.4 us)
Async XLA Ops:
  7.2 104.9 %all-gather.8.cloned.1.call-start = ((), (), s32[]{:S(2)}) async-start(), calls=%async_computation.7 | async-start | bytes 2359296 | tf_op jit(solution)/shard_map/all_gather | solution.py:161
  7.9 158.7 %all-gather.10.cloned.1.call-start = ((), (), s32[]{:S(2)}) async-start(), calls=%async_computation.8 | async-start | bytes 2359296 | tf_op jit(solution)/shard_map/all_gather | solution.py:164
  8.7 315.8 %all-reduce.12.cloned.1.call-start = ((), (), s32[]{:S(2)}) async-start(), calls=%async_computation.9 | async-start | bytes 16777216 | tf_op jit(solution)/shard_map/psum | solution.py:193
  14.6 96.5 %copy-start.37 = (f32[1024]{0:T(1024)}, f32[1024]{0:T(1024)S(1)}, u32[]{:S(2)}) copy-start(f32[1024]{0:T(1024)S(1)} %fusion.50) | copy-start | bytes 12292
  38.0 73.1 %copy-start.33 = (f32[8,1,256]{2,1,0:T(1,128)}, f32[8,1,256]{2,1,0:T(1,128)S(1)}, u32[]{:S(2)}) copy-start(f32[8,1,256]{2,1,0:T(1,128)S(1)} %convert_element_type.247) | copy-start | bytes 24580
  38.6 65.6 %copy-start.26 = (f32[1,1024,32]{1,2,0:T(8,128)}, f32[1,1024,32]{1,2,0:T(8,128)S(1)}, u32[]{:S(2)}) copy-start(f32[1,1024,32]{1,2,0:T(8,128)S(1)} %get-tuple-element.87) | copy-start | bytes 393220
  38.6 65.6 %copy-start.28 = (f32[1,1024,32]{1,2,0:T(8,128)}, f32[1,1024,32]{1,2,0:T(8,128)S(1)}, u32[]{:S(2)}) copy-start(f32[1,1024,32]{1,2,0:T(8,128)S(1)} %get-tuple-element.88) | copy-start | bytes 393220
  38.6 79.0 %copy-start.24 = (f32[1024,64]{0,1:T(8,128)}, f32[1024,64]{0,1:T(8,128)S(1)}, u32[]{:S(2)}) copy-start(f32[1024,64]{0,1:T(8,128)S(1)} %maximum_bitcast_fusion) | copy-start | bytes 786436
  38.7 78.9 %copy-start.22 = (f32[1024,64]{0,1:T(8,128)}, f32[1024,64]{0,1:T(8,128)S(1)}, u32[]{:S(2)}) copy-start(f32[1024,64]{0,1:T(8,128)S(1)} %maximum_bitcast_fusion.1) | copy-start | bytes 786436
  71.8 39.3 %copy-start.15 = (bf16[2048,128]{1,0:T(8,128)(2,1)}, bf16[2048,128]{1,0:T(8,128)(2,1)S(1)}, u32[]{:S(2)}) copy-start(bf16[2048,128]{1,0:T(8,128)(2,1)S(1)} %all_gather.29) | copy-start | bytes 1572868
  111.9 48.3 %copy-start.8 = (pred[512,1024]{0,1:T(8,128)(4,1)}, pred[512,1024]{0,1:T(8,128)(4,1)S(1)}, u32[]{:S(2)}) copy-start(pred[512,1024]{0,1:T(8,128)(4,1)S(1)} %get-tuple-element.89) | copy-start | bytes 1572868
  112.0 23.2 %copy-start.11 = (bf16[1024,2,64,1]{0,2,3,1:T(8,128)(2,1)}, bf16[1024,2,64,1]{0,2,3,1:T(8,128)(2,1)S(1)}, u32[]{:S(2)}) copy-start(bf16[1024,2,64,1]{0,2,3,1:T(8,128)(2,1)S(1)} %fusion.46) | copy-start | bytes 786436
  118.3 17.0 copy-start.17
  174.2 276.9 %all-gather.14.cloned.1.call-start = ((), (), s32[]{:S(2)}) async-start(), calls=%async_computation.11 | async-start | bytes 9437184 | tf_op jit(solution)/shard_map/all_gather | solution.py:167
  174.8 401.0 %all-gather.12.cloned.1.call-start = ((), (), s32[]{:S(2)}) async-start(), calls=%async_computation.10 | async-start | bytes 9437184 | tf_op jit(solution)/shard_map/all_gather | solution.py:166
  175.4 525.4 %all-gather.16.cloned.1.call-start = ((), (), s32[]{:S(2)}) async-start(), calls=%async_computation.12 | async-start | bytes 9437184 | tf_op jit(solution)/shard_map/all_gather | solution.py:168
  176.0 724.6 %all-reduce.14.cloned.1.call-start = ((), (), s32[]{:S(2)}) async-start(), calls=%async_computation.13 | async-start | bytes 16777216 | tf_op jit(solution)/shard_map/psum | solution.py:211
  749.4 346.3 %reduce-scatter.12.cloned.1.call-start = ((), (), s32[]{:S(2)}) async-start(), calls=%async_computation.16 | async-start | bytes 589824 | tf_op jit(solution)/shard_map/reduce_scatter | solution.py:260
  908.5 16.3 slice-start
  908.5 16.3 slice-start.1
  964.6 132.6 %reduce-scatter.10.cloned.1.call-start = ((), (), s32[]{:S(2)}) async-start(), calls=%async_computation.15 | async-start | bytes 589824 | tf_op jit(solution)/shard_map/reduce_scatter | solution.py:257
  964.7 30.0 %copy-start.20 = (bf16[1,512,8,64]{1,3,2,0:T(8,128)(2,1)S(1)}, bf16[1,512,8,64]{1,3,2,0:T(8,128)(2,1)}, u32[]{:S(2)}) copy-start(bf16[1,512,8,64]{1,3,2,0:T(8,128)(2,1)} %copy-done.19) | copy-start | bytes 1572868
  1006.0 159.3 %reduce-scatter.14.cloned.1.call-start = ((), (), s32[]{:S(2)}) async-start(), calls=%async_computation.17 | async-start | bytes 2359296 | tf_op jit(solution)/shard_map/reduce_scatter | solution.py:263
  1013.1 223.7 %reduce-scatter.8.cloned.1.call-start = ((), (), s32[]{:S(2)}) async-start(), calls=%async_computation.14 | async-start | bytes 2359296 | tf_op jit(solution)/shard_map/reduce_scatter | solution.py:254
  1029.5 362.2 %all-reduce.16.cloned.1.call-start = ((), (), s32[]{:S(2)}) async-start(), calls=%async_computation.21 | async-start | bytes 16777216 | tf_op jit(solution)/shard_map/psum | solution.py:200
  1050.7 493.1 %reduce-scatter.20.cloned.1.call-start = ((), (), s32[]{:S(2)}) async-start(), calls=%async_computation.20 | async-start | bytes 9437184 | tf_op jit(solution)/shard_map/reduce_scatter | solution.py:275
  1065.2 628.8 %reduce-scatter.18.cloned.1.call-start = ((), (), s32[]{:S(2)}) async-start(), calls=%async_computation.19 | async-start | bytes 9437184 | tf_op jit(solution)/shard_map/reduce_scatter | solution.py:272
  1079.3 764.7 %reduce-scatter.16.cloned.1.call-start = ((), (), s32[]{:S(2)}) async-start(), calls=%async_computation.18 | async-start | bytes 9437184 | tf_op jit(solution)/shard_map/reduce_scatter | solution.py:269
  1093.8 298.0 %copy-start.34 = (f32[8,1,256]{2,1,0:T(1,128)S(1)}, f32[8,1,256]{2,1,0:T(1,128)}, u32[]{:S(2)}) copy-start(f32[8,1,256]{2,1,0:T(1,128)} %copy-done.33) | copy-start | bytes 24580
  1093.8 298.0 %copy-start.38 = (f32[1024]{0:T(1024)S(1)}, f32[1024]{0:T(1024)}, u32[]{:S(2)}) copy-start(f32[1024]{0:T(1024)} %copy-done.37) | copy-start | bytes 12292
  1093.8 303.9 %copy-start.41 = (bf16[2048]{0:T(1024)(128)(2,1)S(1)}, bf16[2048]{0:T(1024)(128)(2,1)}, u32[]{:S(2)}) copy-start(bf16[2048]{0:T(1024)(128)(2,1)} %get-tuple-element.52) | copy-start | bytes 12292
  1093.8 328.1 %copy-start.40 = (f32[1024]{0:T(1024)S(1)}, f32[1024]{0:T(1024)}, u32[]{:S(2)}) copy-start(f32[1024]{0:T(1024)} %copy-done.39) | copy-start | bytes 12292
  (39 other events, 255.5 us)
Sparse Core Ops, SparseCore 0:
  10.1 57.9 all-gather.7
  70.1 52.7 all-gather.9
  174.3 150.0 all-reduce.11
  326.4 124.6 all-gather.13
  453.1 122.6 all-gather.11
  577.7 123.1 all-gather.15
  749.5 151.0 all-reduce.13
  964.7 62.7 reduce-scatter.11
  1031.5 61.6 reduce-scatter.9
  1097.1 68.1 reduce-scatter.13
  1169.4 67.4 reduce-scatter.7
  1239.8 151.8 all-reduce.15
  1395.4 148.4 reduce-scatter.19
  1547.3 146.5 reduce-scatter.17
  1697.4 146.5 reduce-scatter.15
where the time goes:
time: 1860 us; the launch traced here: 1850 us
  waiting for transfers between devices  1310 us (70%)
  matrix products  262 us (14%)
  blocking collectives  127 us (7%)
  other arithmetic  124 us (7%)
    psum x1, waiting for transfers between devices, shards(): lax.psum(ffn_part.astype(jnp.bfloat16), 'tensor').astype(jnp.float32)  153 us
    psum x1, waiting for transfers between devices, shards(): normed_two_grad = lax.psum(mlp_part, 'tensor')  150 us
    reduce_scatter x1, waiting for transfers between devices, shards(): lax.psum_scatter(up_weight_grad.astype(jnp.bfloat16), 'dp', scatter_dimen...  147 us
    reduce_scatter x1, waiting for transfers between devices, shards(): lax.psum_scatter(gate_weight_grad.astype(jnp.bfloat16), 'dp', scatter_dim...  147 us
    psum x1, waiting for transfers between devices, shards(): hidden_state = tokens_float + lax.psum(attn_part, 'tensor')  132 us
    all_gather x1, waiting for transfers between devices, shards(): lax.all_gather(up_weight, 'dp', axis=0, tiled=True)  115 us
    all_gather x1, waiting for transfers between devices, shards(): lax.all_gather(down_weight, 'dp', axis=1, tiled=True)  110 us
    all_gather x1, waiting for transfers between devices, shards(): lax.all_gather(gate_weight, 'dp', axis=0, tiled=True)  110 us
  transfers between devices with their start and end apart: 15, of which 11 were waited for; matrix products, arithmetic and copies ran while one was open for 14% of the time, Pallas kernels for 0%

commit v1 on v0

--- a/solution.py
+++ b/solution.py
@@ -208,7 +208,11 @@
     gate_weight_grad = contract_rows(normed_two, gate_low)
     up_weight_grad = contract_rows(normed_two, up_low)
     mlp_part = contract_cols(gate_low, gathered[6]) + contract_cols(up_low, gathered[7])
-    normed_two_grad = lax.psum(mlp_part, "tensor")
+    normed_two_grad = mlp_part
+    for hop in (1, 2):
+        normed_two_grad = normed_two_grad + lax.ppermute(
+            normed_two_grad, "tensor", [(dev, dev ^ hop) for dev in range(4)]
+        )
     unused_second, second_pull = jax.vjp(rms_norm, hidden_state, ffn_scale)
     hidden_part, ffn_gain_grad = second_pull(normed_two_grad)
     hidden_grad = cotangent_float + hidden_part

time: 1860 us -> 1630 us (0.88)
  waiting for transfers between devices: 1310 us -> 1050 us
  other arithmetic: 124 us -> 144 us
    ppermute x0 -> x2, waiting for transfers between devices: none -> 180 us  [shards(): lax.ppermute(normed_two_grad, 'tensor', [(dev, dev ^ hop) for dev in rang...]
    psum x1 -> x0, waiting for transfers between devices: 150 us -> none  [shards(): normed_two_grad = lax.psum(mlp_part, 'tensor')]
    reduce_scatter x1, waiting for transfers between devices: 147 us -> 0.02 us  [shards(): lax.psum_scatter(up_weight_grad.astype(jnp.bfloat16), 'dp', scatter_dimen...]
    reduce_scatter x1, waiting for transfers between devices: 147 us -> 0.01 us  [shards(): lax.psum_scatter(gate_weight_grad.astype(jnp.bfloat16), 'dp', scatter_dim...]
    reduce_scatter x1, waiting for transfers between devices: 106 us -> 23.9 us  [shards(): lax.psum_scatter(down_grad.astype(jnp.bfloat16), 'dp', scatter_dimension=...]
    reduce_scatter x1, waiting for transfers between devices: 0.01 us -> 64.1 us  [shards(): lax.psum_scatter(key_weight_grad.astype(jnp.bfloat16), 'dp', scatter_dime...]
    reduce_scatter x1, waiting for transfers between devices: 0.02 us -> 62.8 us  [shards(): lax.psum_scatter(value_weight_grad.astype(jnp.bfloat16), 'dp', scatter_di...]
    reduce_scatter x1, waiting for transfers between devices: 69.8 us -> 27.2 us  [shards(): lax.psum_scatter(query_weight_grad.astype(jnp.bfloat16), 'dp', scatter_di...]
  transfers between devices with their start and end apart: 15 -> 16, of which waited for: 11 -> 12; matrix products, arithmetic and copies ran while one was open for 14% -> 23% of each run, Pallas kernels for 0% -> 0%
where the time goes in v1:
time: 1630 us; the launch traced here: 1620 us
  waiting for transfers between devices  1050 us (64%)
  matrix products  267 us (16%)
  other arithmetic  144 us (9%)
  blocking collectives  126 us (8%)
    ppermute x2, waiting for transfers between devices, shards(): lax.ppermute(normed_two_grad, 'tensor', [(dev, dev ^ hop) for dev in rang...  180 us
    psum x1, waiting for transfers between devices, shards(): lax.psum(ffn_part.astype(jnp.bfloat16), 'tensor').astype(jnp.float32)  153 us
    psum x1, waiting for transfers between devices, shards(): hidden_state = tokens_float + lax.psum(attn_part, 'tensor')  132 us
    all_gather x1, waiting for transfers between devices, shards(): lax.all_gather(up_weight, 'dp', axis=0, tiled=True)  115 us
    all_gather x1, waiting for transfers between devices, shards(): lax.all_gather(down_weight, 'dp', axis=1, tiled=True)  111 us
    all_gather x1, waiting for transfers between devices, shards(): lax.all_gather(gate_weight, 'dp', axis=0, tiled=True)  110 us
    reduce_scatter x1, waiting for transfers between devices, shards(): lax.psum_scatter(output_weight_grad.astype(jnp.bfloat16), 'dp', scatter_d...  69.8 us
    reduce_scatter x1, waiting for transfers between devices, shards(): lax.psum_scatter(key_weight_grad.astype(jnp.bfloat16), 'dp', scatter_dime...  64.1 us
  transfers between devices with their start and end apart: 16, of which 12 were waited for; matrix products, arithmetic and copies ran while one was open for 23% of the time, Pallas kernels for 0%

profile of v1, /device:TPU:0, one launch (start us, length us, event | category | flops | bytes accessed | tf_op | source)
XLA Modules:
  0.0 1621.4 jit_solution(9338486502861592312)
XLA Ops:
  15.5 22.5 %all-gather = bf16[8,1,256]{2,1,0:T(2,128)(2,1)S(1)} all-gather(bf16[1,1,256]{2,1,0:T(2,128)(2,1)S(1)} %reshape.443), channel_id=1, replica_groups=mesh['dp'=8,'tensor'=4] {'dp'}, dimensions={0}, use_global_device_ids=true | all-gather | bytes 4608 | tf_op jit(solution)/shard_map/all_gather | solution.py:160
  38.7 33.1 %all_gather.29 = bf16[2048,128]{1,0:T(8,128)(2,1)S(1)} all-gather(bf16[256,128]{1,0:T(8,128)(2,1)} %param.16), channel_id=1, replica_groups=mesh['dp'=8,'tensor'=4] {'dp'}, dimensions={0}, use_global_device_ids=true | all-gather | bytes 589824 | tf_op jit(solution)/shard_map/all_gather | solution.py:162
  71.8 32.3 %all_gather.28 = bf16[2048,128]{1,0:T(8,128)(2,1)S(1)} all-gather(bf16[256,128]{1,0:T(8,128)(2,1)} %param.17), channel_id=1, replica_groups=mesh['dp'=8,'tensor'=4] {'dp'}, dimensions={0}, use_global_device_ids=true | all-gather | bytes 589824 | tf_op jit(solution)/shard_map/all_gather | solution.py:163
  176.2 16.3 %all-gather.1 = bf16[8,1,256]{2,1,0:T(2,128)(2,1)S(1)} all-gather(bf16[1,1,256]{2,1,0:T(2,128)(2,1)S(1)} %reshape.445), channel_id=1, replica_groups=mesh['dp'=8,'tensor'=4] {'dp'}, dimensions={0}, use_global_device_ids=true | all-gather | bytes 4608 | tf_op jit(solution)/shard_map/all_gather | solution.py:165
  192.5 132.1 %all-reduce.11.cloned.1.call-done = f32[1024,2048]{1,0:T(8,128)} async-done(((f32[1024,2048]{1,0:T(8,128)}), f32[1024,2048]{1,0:T(8,128)}) %all-reduce.11.cloned.1.call-update) | async-done | bytes 8388624 | tf_op jit(solution)/shard_map/psum | solution.py:193
  336.5 114.8 %all-gather.14.cloned.1.call-done = bf16[2048,2048]{1,0:T(8,128)(2,1)} async-done(((bf16[256,2048]{1,0:T(8,128)(2,1)}), bf16[2048,2048]{1,0:T(8,128)(2,1)}) %all-gather.14.cloned.1.call-update) | async-done | bytes 8388624 | tf_op jit(solution)/shard_map/all_gather | solution.py:167
  451.2 14.6 fusion.66
  465.9 110.0 %all-gather.12.cloned.1.call-done = bf16[2048,2048]{1,0:T(8,128)(2,1)} async-done(((bf16[256,2048]{1,0:T(8,128)(2,1)}), bf16[2048,2048]{1,0:T(8,128)(2,1)}) %all-gather.12.cloned.1.call-update) | async-done | bytes 8388624 | tf_op jit(solution)/shard_map/all_gather | solution.py:166
  575.9 14.5 fusion.65
  590.4 110.6 %all-gather.16.cloned.1.call-done = bf16[2048,2048]{1,0:T(8,128)(2,1)} async-done(((bf16[2048,256]{1,0:T(8,128)(2,1)}), bf16[2048,2048]{1,0:T(8,128)(2,1)}) %all-gather.16.cloned.1.call-update) | async-done | bytes 8388624 | tf_op jit(solution)/shard_map/all_gather | solution.py:168
  701.0 21.7 %multiply_convert_fusion = (bf16[1024,2048]{1,0:T(8,128)(2,1)}, bf16[1024,2048]{1,0:T(8,128)(2,1)}, bf16[1024,2048]{1,0:T(8,128)(2,1)}) fusion(f32[1024,2048]{1,0:T(8,128)} %fusion.65, f32[1024,2048]{1,0:T(8,128)} %fusion.66, bf16[1024,2048]{1,0:T(8,128)(2,1)} %param.23, bf16[2048,2048]{1,0:T(8,128)(2,1)} %all-gather.16.cloned.1.call-done), kind=kOutput, calls=%fused_computation.44 | convolution fusion | flops 8623489024 | bytes 41943040 | tf_op jit(solution)/shard_map/dot_general | solution.py:61
  722.6 14.5 convolution_convert_fusion.1
  737.2 14.1 convolution_convert_fusion.2
  751.4 12.8 fusion.67
  764.2 12.7 convolution_add_fusion
  780.3 13.3 collective-permute-done
  793.6 12.0 add.176
  807.1 13.5 convolution_convert_fusion
  821.6 166.7 %collective-permute-done.1 = f32[1024,2048]{1,0:T(8,128)} collective-permute-done((f32[1024,2048]{1,0:T(8,128)}, f32[1024,2048]{1,0:T(8,128)}, u32[]{:S(2)}, u32[]{:S(2)}) %collective-permute-start.1) | collective-permute-done | bytes 8388640 | tf_op jit(solution)/shard_map/ppermute | solution.py:213
  988.3 10.7 multiply_reduce_fusion
  999.1 14.8 fusion.17
  1036.8 12.2 fusion.3
  1049.0 11.9 fusion
  1060.9 30.9 %fusion.2 = (bf16[2,4,512,1024]{2,3,1,0:T(8,128)(2,1)}, bf16[2,4,512,1024]{2,3,1,0:T(8,128)(2,1)}) fusion(f32[2,1024,512,4]{2,1,3,0:T(8,128)} %get-tuple-element.98, f32[2,1024,512,4]{2,1,3,0:T(8,128)} %get-tuple-element.94, f32[2,4,512]{2,1,0:T(4,128)S(1)} %get-tuple-element.97, f32[2,4,512]{2,1,0:T(4,128)S(1)} %bitcast.237, ...), kind=kLoop, calls=%fused_computation.4 | loop fusion | flops 50331648 | bytes 85000192 | tf_op jit(solution)/shard_map/while/body/eval_jaxpr/convert_element_type | solution.py:123
  1114.2 14.0 convolution_convert_fusion.3
  1159.9 23.9 %reduce-scatter.20.cloned.1.call-done = bf16[2048,256]{1,0:T(8,128)(2,1)} async-done(((bf16[2048,2048]{1,0:T(8,128)(2,1)}), bf16[2048,256]{1,0:T(8,128)(2,1)}) %reduce-scatter.20.cloned.1.call-update) | async-done | bytes 1048592 | tf_op jit(solution)/shard_map/reduce_scatter | solution.py:279
  1186.5 62.8 %reduce-scatter.12.cloned.1.call-done = bf16[256,128]{1,0:T(8,128)(2,1)} async-done(((bf16[2048,128]{1,0:T(8,128)(2,1)}), bf16[256,128]{1,0:T(8,128)(2,1)}) %reduce-scatter.12.cloned.1.call-update) | async-done | bytes 65552 | tf_op jit(solution)/shard_map/reduce_scatter | solution.py:264
  1250.8 64.1 %reduce-scatter.10.cloned.1.call-done = bf16[256,128]{1,0:T(8,128)(2,1)} async-done(((bf16[2048,128]{1,0:T(8,128)(2,1)}), bf16[256,128]{1,0:T(8,128)(2,1)}) %reduce-scatter.10.cloned.1.call-update) | async-done | bytes 65552 | tf_op jit(solution)/shard_map/reduce_scatter | solution.py:261
  1316.5 69.8 %reduce-scatter.14.cloned.1.call-done = bf16[512,256]{1,0:T(8,128)(2,1)} async-done(((bf16[512,2048]{1,0:T(8,128)(2,1)}), bf16[512,256]{1,0:T(8,128)(2,1)}) %reduce-scatter.14.cloned.1.call-update) | async-done | bytes 262160 | tf_op jit(solution)/shard_map/reduce_scatter | solution.py:267
  1388.1 152.8 %all-reduce.13.cloned.1.call-done = (bf16[1024,2048]{1,0:T(8,128)(2,1)}, bf16[1024,2048]{1,0:T(8,128)(2,1)}) async-done(((bf16[1024,2048]{1,0:T(8,128)(2,1)}, bf16[1024,2048]{1,0:T(8,128)(2,1)}), (bf16[1024,2048]{1,0:T(8,128)(2,1)}, bf16[1024,2048]{1,0:T(8,128)(2,1)})) %all-reduce.13.cloned.1.call-update) | async-done | bytes 8388624 | tf_op jit(solution)/shard_map/psum | solution.py:200
  1546.8 22.1 %all-reduce.6 = (bf16[2048]{0:T(1024)(128)(2,1)S(1)}, bf16[2048]{0:T(1024)(128)(2,1)S(1)}) all-reduce(bf16[2048]{0:T(1024)(128)(2,1)S(1)} %get-tuple-element.54, bf16[2048]{0:T(1024)(128)(2,1)S(1)} %get-tuple-element.52), channel_id=2, replica_groups=mesh['dp'=8,'tensor'=4] {'dp'}, use_global_device_ids=true, to_apply=%region_16.17.clone | all-reduce | flops 4096 | bytes 16384
  1585.6 27.2 %reduce-scatter.8.cloned.1.call-done = bf16[256,512]{1,0:T(8,128)(2,1)} async-done(((bf16[2048,512]{1,0:T(8,128)(2,1)}), bf16[256,512]{1,0:T(8,128)(2,1)}) %reduce-scatter.8.cloned.1.call-update) | async-done | bytes 262160 | tf_op jit(solution)/shard_map/reduce_scatter | solution.py:258
  (242 shorter events, 206.1 us)
Async XLA Ops:
  7.2 104.9 %all-gather.8.cloned.1.call-start = ((), (), s32[]{:S(2)}) async-start(), calls=%async_computation.7 | async-start | bytes 2359296 | tf_op jit(solution)/shard_map/all_gather | solution.py:161
  7.9 158.9 %all-gather.10.cloned.1.call-start = ((), (), s32[]{:S(2)}) async-start(), calls=%async_computation.8 | async-start | bytes 2359296 | tf_op jit(solution)/shard_map/all_gather | solution.py:164
  8.7 315.9 %all-reduce.11.cloned.1.call-start = ((), (), s32[]{:S(2)}) async-start(), calls=%async_computation.9 | async-start | bytes 16777216 | tf_op jit(solution)/shard_map/psum | solution.py:193
  14.6 96.5 %copy-start.46 = (f32[1024]{0:T(1024)}, f32[1024]{0:T(1024)S(1)}, u32[]{:S(2)}) copy-start(f32[1024]{0:T(1024)S(1)} %fusion.50) | copy-start | bytes 12292
  38.0 73.1 %copy-start.39 = (f32[8,1,256]{2,1,0:T(1,128)}, f32[8,1,256]{2,1,0:T(1,128)S(1)}, u32[]{:S(2)}) copy-start(f32[8,1,256]{2,1,0:T(1,128)S(1)} %convert_element_type.247) | copy-start | bytes 24580
  38.6 65.6 %copy-start.29 = (f32[1,1024,32]{1,2,0:T(8,128)}, f32[1,1024,32]{1,2,0:T(8,128)S(1)}, u32[]{:S(2)}) copy-start(f32[1,1024,32]{1,2,0:T(8,128)S(1)} %get-tuple-element.87) | copy-start | bytes 393220
  38.6 65.6 %copy-start.31 = (f32[1,1024,32]{1,2,0:T(8,128)}, f32[1,1024,32]{1,2,0:T(8,128)S(1)}, u32[]{:S(2)}) copy-start(f32[1,1024,32]{1,2,0:T(8,128)S(1)} %get-tuple-element.88) | copy-start | bytes 393220
  38.6 79.1 %copy-start.25 = (f32[1024,64]{0,1:T(8,128)}, f32[1024,64]{0,1:T(8,128)S(1)}, u32[]{:S(2)}) copy-start(f32[1024,64]{0,1:T(8,128)S(1)} %maximum_bitcast_fusion) | copy-start | bytes 786436
  38.7 79.1 %copy-start.23 = (f32[1024,64]{0,1:T(8,128)}, f32[1024,64]{0,1:T(8,128)S(1)}, u32[]{:S(2)}) copy-start(f32[1024,64]{0,1:T(8,128)S(1)} %maximum_bitcast_fusion.1) | copy-start | bytes 786436
  109.6 50.7 %copy-start.27 = (bf16[1024,128]{0,1:T(8,128)(2,1)}, bf16[1024,128]{0,1:T(8,128)(2,1)S(1)}, u32[]{:S(2)}) copy-start(bf16[1024,128]{0,1:T(8,128)(2,1)S(1)} %convolution_convert_fusion.10) | copy-start | bytes 786436
  111.9 40.1 %copy-start.8 = (pred[512,1024]{0,1:T(8,128)(4,1)}, pred[512,1024]{0,1:T(8,128)(4,1)S(1)}, u32[]{:S(2)}) copy-start(pred[512,1024]{0,1:T(8,128)(4,1)S(1)} %get-tuple-element.90) | copy-start | bytes 1572868
  111.9 48.4 %copy-start.6 = (pred[512,1024]{0,1:T(8,128)(4,1)}, pred[512,1024]{0,1:T(8,128)(4,1)S(1)}, u32[]{:S(2)}) copy-start(pred[512,1024]{0,1:T(8,128)(4,1)S(1)} %get-tuple-element.89) | copy-start | bytes 1572868
  174.4 276.9 %all-gather.14.cloned.1.call-start = ((), (), s32[]{:S(2)}) async-start(), calls=%async_computation.11 | async-start | bytes 9437184 | tf_op jit(solution)/shard_map/all_gather | solution.py:167
  175.0 400.9 %all-gather.12.cloned.1.call-start = ((), (), s32[]{:S(2)}) async-start(), calls=%async_computation.10 | async-start | bytes 9437184 | tf_op jit(solution)/shard_map/all_gather | solution.py:166
  175.5 525.4 %all-gather.16.cloned.1.call-start = ((), (), s32[]{:S(2)}) async-start(), calls=%async_computation.12 | async-start | bytes 9437184 | tf_op jit(solution)/shard_map/all_gather | solution.py:168
  176.1 978.2 %reduce-scatter.18.cloned.1.call-start = ((), (), s32[]{:S(2)}) async-start(), calls=%async_computation.18 | async-start | bytes 9437184 | tf_op jit(solution)/shard_map/reduce_scatter | solution.py:276
  192.5 138.4 %copy-start.41 = (f32[8,1,256]{2,1,0:T(1,128)}, f32[8,1,256]{2,1,0:T(1,128)S(1)}, u32[]{:S(2)}) copy-start(f32[8,1,256]{2,1,0:T(1,128)S(1)} %convert_element_type.248) | copy-start | bytes 24580
  737.1 420.0 %reduce-scatter.16.cloned.1.call-start = ((), (), s32[]{:S(2)}) async-start(), calls=%async_computation.17 | async-start | bytes 9437184 | tf_op jit(solution)/shard_map/reduce_scatter | solution.py:273
  751.3 432.4 %reduce-scatter.20.cloned.1.call-start = ((), (), s32[]{:S(2)}) async-start(), calls=%async_computation.19 | async-start | bytes 9437184 | tf_op jit(solution)/shard_map/reduce_scatter | solution.py:279
  780.3 13.3 collective-permute-start
  805.6 182.8 %collective-permute-start.1 = (f32[1024,2048]{1,0:T(8,128)}, f32[1024,2048]{1,0:T(8,128)}, u32[]{:S(2)}, u32[]{:S(2)}) collective-permute-start(f32[1024,2048]{1,0:T(8,128)} %add.176), channel_id=1, source_target_pairs={{0,2},{1,3},{2,0},{3,1},{4,6},{5,7},{6,4},{7,5},{8,10},{9,11},{10,... | collective-permute-start | bytes 25165832 | tf_op jit(solution)/shard_map/ppermute | solution.py:213
  820.5 167.8 %copy-start.42 = (f32[8,1,256]{2,1,0:T(1,128)S(1)}, f32[8,1,256]{2,1,0:T(1,128)}, u32[]{:S(2)}) copy-start(f32[8,1,256]{2,1,0:T(1,128)} %copy-done.41) | copy-start | bytes 24580
  820.5 167.8 %copy-start.44 = (f32[1024]{0:T(1024)S(1)}, f32[1024]{0:T(1024)}, u32[]{:S(2)}) copy-start(f32[1024]{0:T(1024)} %copy-done.43) | copy-start | bytes 12292
  820.6 428.7 %reduce-scatter.12.cloned.1.call-start = ((), (), s32[]{:S(2)}) async-start(), calls=%async_computation.15 | async-start | bytes 589824 | tf_op jit(solution)/shard_map/reduce_scatter | solution.py:264
  821.6 177.5 %copy-start.51 = (f32[1024]{0:T(1024)S(1)}, f32[1024]{0:T(1024)}, u32[]{:S(2)}) copy-start(f32[1024]{0:T(1024)} %copy-done.50) | copy-start | bytes 12292
  1098.0 217.0 %reduce-scatter.10.cloned.1.call-start = ((), (), s32[]{:S(2)}) async-start(), calls=%async_computation.14 | async-start | bytes 589824 | tf_op jit(solution)/shard_map/reduce_scatter | solution.py:261
  1106.7 279.6 %reduce-scatter.14.cloned.1.call-start = ((), (), s32[]{:S(2)}) async-start(), calls=%async_computation.16 | async-start | bytes 2359296 | tf_op jit(solution)/shard_map/reduce_scatter | solution.py:267
  1114.1 426.8 %all-reduce.13.cloned.1.call-start = ((), (), s32[]{:S(2)}) async-start(), calls=%async_computation.20 | async-start | bytes 16777216 | tf_op jit(solution)/shard_map/psum | solution.py:200
  1146.8 466.0 %reduce-scatter.8.cloned.1.call-start = ((), (), s32[]{:S(2)}) async-start(), calls=%async_computation.13 | async-start | bytes 2359296 | tf_op jit(solution)/shard_map/reduce_scatter | solution.py:258
  1153.0 387.9 %copy-start.40 = (f32[8,1,256]{2,1,0:T(1,128)S(1)}, f32[8,1,256]{2,1,0:T(1,128)}, u32[]{:S(2)}) copy-start(f32[8,1,256]{2,1,0:T(1,128)} %copy-done.39) | copy-start | bytes 24580
  1153.0 387.9 %copy-start.47 = (f32[1024]{0:T(1024)S(1)}, f32[1024]{0:T(1024)}, u32[]{:S(2)}) copy-start(f32[1024]{0:T(1024)} %copy-done.46) | copy-start | bytes 12292
  1157.1 413.1 %copy-start.49 = (f32[1024]{0:T(1024)S(1)}, f32[1024]{0:T(1024)}, u32[]{:S(2)}) copy-start(f32[1024]{0:T(1024)} %copy-done.48) | copy-start | bytes 12292
  (47 other events, 443.9 us)
Sparse Core Ops, SparseCore 0:
  10.1 57.9 all-gather.7
  70.1 52.7 all-gather.9
  174.5 150.0 all-reduce.10
  326.6 124.6 all-gather.13
  453.2 122.6 all-gather.11
  577.8 123.1 all-gather.15
  737.3 145.6 reduce-scatter.17
  886.5 146.5 reduce-scatter.15
  1036.8 146.9 reduce-scatter.19
  1187.5 61.7 reduce-scatter.11
  1253.2 61.6 reduce-scatter.9
  1318.3 67.9 reduce-scatter.13
  1388.9 151.9 all-reduce.12
  1544.3 68.4 reduce-scatter.7
